TPU v7x, 256 devices: a whole 4x4x8 slice. The times are simulated.
256 devices in a mesh: band: 32 (over x_hi, z, core), fft: 8 (over x_lo, y).
Axes of the slice: x: 4 (x_hi: 2, x_lo: 2; x = x_hi * 2 + x_lo), y: 4, z: 8, core: 2. Of those that a mesh axis runs over, the one named last changes fastest.
Arguments:
- orbitals: float32 [64, 64, 4096], P('band', 'fft'), may hold values from -5 to 5
Outputs:
- exchange: float32 [64, 64, 4096], P('band', 'fft')
All inputs are finite; a program needn't handle non-finite values.
Results may differ from a plain program's by a relative error of at most 0.00018.
Values sent between devices are 32-bit elements; how exact they have to be, the bound alone decides.
No kernel may reach another device: no remote copies, remote signals or barrier semaphores. Data moves between devices by JAX's collectives and lax.ppermute only.
A program may use at most 64 MiB of HBM per device.

v0:
```python
import math
import jax
import jax.numpy as jnp
from jax import lax
from jax.sharding import PartitionSpec as P

GRID = 64
ROUNDS = 2
EXX_FRACTION = 0.25
SCREEN = 0.05


def broadcast(block, axis, holder):
    block = jnp.where(lax.axis_index(axis) == holder, block, jnp.zeros_like(block))
    return lax.psum(block, axis)


def angle_tables(length):
    indices = jnp.arange(length, dtype=jnp.int32)
    residue = indices[:, None] * indices[None, :] % length
    angles = residue.astype(jnp.float32) * (2.0 * math.pi / length)
    return (jnp.cos(angles), jnp.sin(angles))


def kernel_block(length, y_offset, y_count):
    indices = jnp.arange(length, dtype=jnp.int32)
    signed = jnp.where(indices < length // 2, indices, indices - length).astype(jnp.float32)
    wavenum = signed * (2.0 * math.pi / length)
    y_indices = y_offset + jnp.arange(y_count, dtype=jnp.int32)
    y_signed = jnp.where(y_indices < length // 2, y_indices, y_indices - length).astype(jnp.float32)
    y_wavenum = y_signed * (2.0 * math.pi / length)
    squares = (
        wavenum[:, None, None] ** 2 + y_wavenum[None, :, None] ** 2 + wavenum[None, None, :] ** 2
    )
    guarded = jnp.where(squares > 0, squares, 1.0)
    kernel = jnp.where(
        squares > 0, (1.0 - jnp.exp(-guarded / (4.0 * SCREEN * SCREEN))) / guarded, 0.0
    )
    kernel = kernel / float(length) ** 3
    return jnp.concatenate([kernel, kernel], -1)


def along_axis(spectrum, dimension, cosine_table, sine_table, direction):
    halfway = spectrum.shape[-1] // 2
    if dimension == 1:
        formula = "nakm,ab->nbkm"
    else:
        formula = "nakm,kb->nabm"
    cos_part = jnp.einsum(formula, spectrum, cosine_table, precision=lax.Precision.HIGHEST)
    sin_part = jnp.einsum(formula, spectrum, sine_table, precision=lax.Precision.HIGHEST)
    rotated = jnp.concatenate([-sin_part[..., halfway:], sin_part[..., :halfway]], -1)
    return cos_part + direction * rotated


def forward_yz(density, cosine_table, sine_table):
    z_matrix = jnp.concatenate([cosine_table, -sine_table], 1)
    spectrum = jnp.einsum("nayz,zc->nayc", density, z_matrix, precision=lax.Precision.HIGHEST)
    return along_axis(spectrum, 2, cosine_table, sine_table, -1.0)


def inverse_yz(spectrum, cosine_table, sine_table):
    spectrum = along_axis(spectrum, 2, cosine_table, sine_table, 1.0)
    z_matrix = jnp.concatenate([cosine_table, -sine_table], 0)
    return jnp.einsum("nayc,cz->nayz", spectrum, z_matrix, precision=lax.Precision.HIGHEST)


def per_device(orbitals):
    owned_count, planes, flat_cells = orbitals.shape
    length = GRID
    cosine_table, sine_table = angle_tables(length)
    received = []
    for source_round in range(ROUNDS):
        received.append(broadcast(orbitals, "band", source_round))
    kernel_slab = kernel_block(length, lax.axis_index("fft") * planes, planes)
    accumulated = jnp.zeros((owned_count, planes, flat_cells), jnp.float32)
    for sources in received:
        density = (orbitals[:, None] * sources[None]).reshape(
            owned_count * owned_count, planes, length, length
        )
        spectrum = forward_yz(density, cosine_table, sine_table)
        filtered = (
            along_axis(
                lax.all_to_all(spectrum, "fft", split_axis=2, concat_axis=1, tiled=True),
                1,
                cosine_table,
                sine_table,
                -1.0,
            )
            * kernel_slab
        )
        filtered = along_axis(filtered, 1, cosine_table, sine_table, 1.0)
        returned = lax.all_to_all(filtered, "fft", split_axis=1, concat_axis=2, tiled=True)
        potential = inverse_yz(returned, cosine_table, sine_table)
        potential = potential.reshape(owned_count, owned_count, planes, flat_cells)
        accumulated = accumulated + jnp.sum(potential * sources[None], axis=1)
    return -EXX_FRACTION * accumulated


def solution(mesh):
    return jax.shard_map(
        per_device,
        mesh=mesh,
        in_specs=(P("band", "fft", None),),
        out_specs=P("band", "fft", None),
        check_vma=False,
    )
```

profile of v0, /device:TPU:1, one launch (start us, length us, event | category | flops | bytes accessed | tf_op | source)
XLA Modules:
  0.0 377.4 jit_solution(17171705458724565237)
XLA Ops:
  6.5 1.8 broadcast_select_fusion
  9.1 273.8 %all-reduce.3.cloned.1.call-done = (f32[2,8,4096]{2,1,0:T(8,128)}, f32[2,8,4096]{2,1,0:T(8,128)}) async-done(((f32[2,8,4096]{2,1,0:T(8,128)}, f32[2,8,4096]{2,1,0:T(8,128)}), (f32[2,8,4096]{2,1,0:T(8,128)}, f32[2,8,4096]{2,1,0:T(8,128)})) %all-reduce.3.cloned.1.call-update) | async-done | bytes 524304 | tf_op jit(solution)/shard_map/psum | solution.py:15
  282.8 1.1 broadcast_multiply_fusion
  285.4 1.2 convolution_bitcast_fusion.14
  287.0 1.4 fusion.9
  288.4 1.6 copy.24
  290.0 4.0 %all-to-all-start = ((f32[4,8,64,128]{3,1,0,2:T(8,128)}), f32[4,8,64,128]{3,1,0,2:T(8,128)S(1)}, u32[]{:S(2)}, u32[]{:S(2)}) async-start(f32[4,8,64,128]{3,1,0,2:T(8,128)} %copy.24), calls=%async_computation | async-start | bytes 2097152 | tf_op jit(solution)/shard_map/all_to_all | solution.py:83
  294.4 1.0 fusion.76
  295.5 1.2 convolution_bitcast_fusion.6
  297.0 1.4 fusion.4
  298.4 1.6 copy.36
  300.0 9.0 %all-to-all-done = f32[4,8,64,128]{3,1,0,2:T(8,128)S(1)} async-done(((f32[4,8,64,128]{3,1,0,2:T(8,128)}), f32[4,8,64,128]{3,1,0,2:T(8,128)S(1)}, u32[]{:S(2)}, u32[]{:S(2)}) %all-to-all-start) | async-done | bytes 1048608 | tf_op jit(solution)/shard_map/all_to_all | solution.py:83
  309.0 3.7 all-to-all-start.2
  312.7 1.2 convolution_bitcast_fusion.12
  314.3 1.5 fusion.8
  315.7 1.2 convolution_bitcast_fusion.10
  317.3 1.3 fusion.6
  318.6 1.6 copy.30
  320.2 7.3 %all-to-all-done.2 = f32[4,8,64,128]{3,1,0,2:T(8,128)S(1)} async-done(((f32[4,8,64,128]{3,1,0,2:T(8,128)}), f32[4,8,64,128]{3,1,0,2:T(8,128)S(1)}, u32[]{:S(2)}, u32[]{:S(2)}) %all-to-all-start.2) | async-done | bytes 1048608 | tf_op jit(solution)/shard_map/all_to_all | solution.py:83
  327.6 3.7 all-to-all-start.1
  331.2 1.2 convolution_bitcast_fusion.4
  332.8 1.5 fusion.3
  334.3 1.2 convolution_bitcast_fusion.2
  335.8 1.3 fusion.1
  337.2 1.6 copy.42
  338.8 7.5 %all-to-all-done.1 = f32[4,64,8,128]{3,2,0,1:T(8,128)S(1)} async-done(((f32[4,64,8,128]{3,2,0,1:T(8,128)}), f32[4,64,8,128]{3,2,0,1:T(8,128)S(1)}, u32[]{:S(2)}, u32[]{:S(2)}) %all-to-all-start.1) | async-done | bytes 1048608 | tf_op jit(solution)/shard_map/all_to_all | solution.py:92
  346.2 3.8 %all-to-all-start.3 = ((f32[4,64,8,128]{3,2,0,1:T(8,128)}), f32[4,64,8,128]{3,2,0,1:T(8,128)S(1)}, u32[]{:S(2)}, u32[]{:S(2)}) async-start(f32[4,64,8,128]{3,2,0,1:T(8,128)} %copy.42), calls=%async_computation.3 | async-start | bytes 2097152 | tf_op jit(solution)/shard_map/all_to_all | solution.py:92
  350.0 1.2 convolution_bitcast_fusion.8
  351.6 1.4 fusion.5
  354.3 10.6 %all-to-all-done.3 = f32[4,64,8,128]{3,2,0,1:T(8,128)S(1)} async-done(((f32[4,64,8,128]{3,2,0,1:T(8,128)}), f32[4,64,8,128]{3,2,0,1:T(8,128)S(1)}, u32[]{:S(2)}, u32[]{:S(2)}) %all-to-all-start.3) | async-done | bytes 1048608 | tf_op jit(solution)/shard_map/all_to_all | solution.py:92
  364.8 1.2 convolution_bitcast_fusion
  366.4 1.4 fusion
  (32 shorter events, 9.7 us)
Async XLA Ops:
  6.5 276.3 %all-reduce.3.cloned.1.call-start = ((), (), s32[]{:S(2)}) async-start(), calls=%async_computation.4 | async-start | bytes 1048576 | tf_op jit(solution)/shard_map/psum | solution.py:15
  8.9 273.9 %copy-start = (f32[2,8,4096]{2,1,0:T(8,128)S(1)}, f32[2,8,4096]{2,1,0:T(8,128)}, u32[]{:S(2)}) copy-start(f32[2,8,4096]{2,1,0:T(8,128)} %param.1) | copy-start | bytes 786436
  290.0 19.0 %all-to-all-start = ((f32[4,8,64,128]{3,1,0,2:T(8,128)}), f32[4,8,64,128]{3,1,0,2:T(8,128)S(1)}, u32[]{:S(2)}, u32[]{:S(2)}) async-start(f32[4,8,64,128]{3,1,0,2:T(8,128)} %copy.24), calls=%async_computation | async-start | bytes 2097152 | tf_op jit(solution)/shard_map/all_to_all | solution.py:83
  309.0 18.6 %all-to-all-start.2 = ((f32[4,8,64,128]{3,1,0,2:T(8,128)}), f32[4,8,64,128]{3,1,0,2:T(8,128)S(1)}, u32[]{:S(2)}, u32[]{:S(2)}) async-start(f32[4,8,64,128]{3,1,0,2:T(8,128)} %copy.36), calls=%async_computation.2 | async-start | bytes 2097152 | tf_op jit(solution)/shard_map/all_to_all | solution.py:83
  327.6 18.6 %all-to-all-start.1 = ((f32[4,64,8,128]{3,2,0,1:T(8,128)}), f32[4,64,8,128]{3,2,0,1:T(8,128)S(1)}, u32[]{:S(2)}, u32[]{:S(2)}) async-start(f32[4,64,8,128]{3,2,0,1:T(8,128)} %copy.30), calls=%async_computation.1 | async-start | bytes 2097152 | tf_op jit(solution)/shard_map/all_to_all | solution.py:92
  346.2 18.6 %all-to-all-start.3 = ((f32[4,64,8,128]{3,2,0,1:T(8,128)}), f32[4,64,8,128]{3,2,0,1:T(8,128)S(1)}, u32[]{:S(2)}, u32[]{:S(2)}) async-start(f32[4,64,8,128]{3,2,0,1:T(8,128)} %copy.42), calls=%async_computation.3 | async-start | bytes 2097152 | tf_op jit(solution)/shard_map/all_to_all | solution.py:92
  368.7 1.0 copy-start.1
  368.7 1.0 copy-start.2
Sparse Core Ops, SparseCore 0:
  10.0 272.8 all-reduce.2
where the time goes:
time: 378 us; the launch traced here: 377 us
  waiting for transfers between devices  308 us (81%)
  matrix products  24.4 us (6%)
  starting transfers between devices  15.2 us (4%)
  between operations  13.7 us (4%)
  local copies, waits for them, and re-layouts  8.6 us (2%)
  other arithmetic  7.43 us (2%)
    psum x1, waiting for transfers between devices, broadcast(): return lax.psum(block, axis)  274 us
    all_to_all x2, waiting for transfers between devices, per_device(): lax.all_to_all(filtered, 'fft', split_axis=1, concat_axis=2, tiled=True)  18 us
    all_to_all x2, waiting for transfers between devices, per_device(): lax.all_to_all(spectrum, 'fft', split_axis=2, concat_axis=1, tiled=True)  16.3 us
    dot_general x8, matrix products, along_axis(): jnp.einsum(formula, spectrum, cosine_table, precision=lax.Precision.HIGHEST)  11.1 us
    dot_general x8, matrix products, along_axis(): jnp.einsum(formula, spectrum, sine_table, precision=lax.Precision.HIGHEST)  9.25 us
    all_to_all x2, starting transfers between devices, per_device(): lax.all_to_all(spectrum, 'fft', split_axis=2, concat_axis=1, tiled=True)  7.75 us
  transfers between devices with their start and end apart: 5, of which 5 were waited for; matrix products, arithmetic and copies ran while one was open for 7% of the time, Pallas kernels for 0%

commit v1 on v0

--- a/solution.py
+++ b/solution.py
@@ -12,7 +12,7 @@
 
 def broadcast(block, axis, holder):
     block = jnp.where(lax.axis_index(axis) == holder, block, jnp.zeros_like(block))
-    return lax.psum(block, axis)
+    return jnp.sum(lax.all_gather(block, axis), axis=0)
 
 
 def angle_tables(length):

time: 378 us -> 313 us (0.83)
  waiting for transfers between devices: 308 us -> 238 us
  other arithmetic: 7.43 us -> 13.9 us
    psum x1 -> x0, waiting for transfers between devices: 274 us -> none  [broadcast(): return lax.psum(block, axis)]
    all_gather x0 -> x2, waiting for transfers between devices: none -> 203 us  [broadcast(): return jnp.sum(lax.all_gather(block, axis), axis=0)]
    reduce_sum x0 -> x2, other arithmetic: none -> 7.61 us  [broadcast(): return jnp.sum(lax.all_gather(block, axis), axis=0)]
  transfers between devices with their start and end apart: 5 -> 6, of which waited for: 5 -> 6; matrix products, arithmetic and copies ran while one was open for 7% -> 9% of each run, Pallas kernels for 0% -> 0%
where the time goes in v1:
time: 313 us
  waiting for transfers between devices  238 us (76%)
  matrix products  24.4 us (8%)
  starting transfers between devices  15.2 us (5%)
  other arithmetic  13.9 us (4%)
  between operations  13.7 us (4%)
  local copies, waits for them, and re-layouts  7.95 us (3%)
    all_gather x2, waiting for transfers between devices, broadcast(): return jnp.sum(lax.all_gather(block, axis), axis=0)  203 us
    all_to_all x2, waiting for transfers between devices, per_device(): lax.all_to_all(filtered, 'fft', split_axis=1, concat_axis=2, tiled=True)  18 us
    all_to_all x2, waiting for transfers between devices, per_device(): lax.all_to_all(spectrum, 'fft', split_axis=2, concat_axis=1, tiled=True)  16.3 us
    dot_general x8, matrix products, along_axis(): jnp.einsum(formula, spectrum, cosine_table, precision=lax.Precision.HIGHEST)  11.1 us
    dot_general x8, matrix products, along_axis(): jnp.einsum(formula, spectrum, sine_table, precision=lax.Precision.HIGHEST)  9.25 us
    all_to_all x2, starting transfers between devices, per_device(): lax.all_to_all(spectrum, 'fft', split_axis=2, concat_axis=1, tiled=True)  7.75 us
    reduce_sum x2, other arithmetic, broadcast(): return jnp.sum(lax.all_gather(block, axis), axis=0)  7.61 us
    all_to_all x2, starting transfers between devices, per_device(): lax.all_to_all(filtered, 'fft', split_axis=1, concat_axis=2, tiled=True)  7.43 us
  transfers between devices with their start and end apart: 6, of which 6 were waited for; matrix products, arithmetic and copies ran while one was open for 9% of the time, Pallas kernels for 0%

profile of v1, /device:TPU:1, one launch (start us, length us, event | category | flops | bytes accessed | tf_op | source)
XLA Modules:
  0.0 312.9 jit_solution(11619242409812966242)
XLA Ops:
  6.5 1.8 broadcast_select_fusion
  9.7 105.9 %all-gather.5.cloned.1.call-done = f32[64,8,4096]{2,1,0:T(8,128)} async-done(((f32[2,8,4096]{2,1,0:T(8,128)}), f32[64,8,4096]{2,1,0:T(8,128)}) %all-gather.5.cloned.1.call-update) | async-done | bytes 8388624 | tf_op jit(solution)/shard_map/all_gather | solution.py:15
  115.5 3.8 %reduce_sum.36 = f32[2,8,4096]{2,1,0:T(8,128)S(1)} reduce(f32[32,2,8,4096]{3,2,1,0:T(8,128)} %bitcast.174, f32[]{:T(128)} %constant.23.clone.1), dimensions={0}, to_apply=%region_0.1 | reduce | flops 2031616 | bytes 8650756 | tf_op jit(solution)/shard_map/reduce_sum | solution.py:15
  119.4 96.9 %all-gather.7.cloned.1.call-done = f32[64,8,4096]{2,1,0:T(8,128)} async-done(((f32[2,8,4096]{2,1,0:T(8,128)}), f32[64,8,4096]{2,1,0:T(8,128)}) %all-gather.7.cloned.1.call-update) | async-done | bytes 8388624 | tf_op jit(solution)/shard_map/all_gather | solution.py:15
  216.2 3.8 %reduce_sum.38 = f32[2,8,4096]{2,1,0:T(8,128)S(1)} reduce(f32[32,2,8,4096]{3,2,1,0:T(8,128)} %bitcast.175, f32[]{:T(128)} %constant.23.clone.1), dimensions={0}, to_apply=%region_2.3 | reduce | flops 2031616 | bytes 8650756 | tf_op jit(solution)/shard_map/reduce_sum | solution.py:15
  221.6 1.2 convolution_bitcast_fusion.6
  223.1 1.4 fusion.4
  224.5 1.6 copy.36
  226.2 4.0 %all-to-all-start.2 = ((f32[4,8,64,128]{3,1,0,2:T(8,128)}), f32[4,8,64,128]{3,1,0,2:T(8,128)S(1)}, u32[]{:S(2)}, u32[]{:S(2)}) async-start(f32[4,8,64,128]{3,1,0,2:T(8,128)} %copy.36), calls=%async_computation.2 | async-start | bytes 2097152 | tf_op jit(solution)/shard_map/all_to_all | solution.py:83
  231.6 1.2 convolution_bitcast_fusion.14
  233.2 1.4 fusion.9
  234.6 1.6 copy.24
  236.2 8.9 %all-to-all-done.2 = f32[4,8,64,128]{3,1,0,2:T(8,128)S(1)} async-done(((f32[4,8,64,128]{3,1,0,2:T(8,128)}), f32[4,8,64,128]{3,1,0,2:T(8,128)S(1)}, u32[]{:S(2)}, u32[]{:S(2)}) %all-to-all-start.2) | async-done | bytes 1048608 | tf_op jit(solution)/shard_map/all_to_all | solution.py:83
  245.1 3.7 %all-to-all-start = ((f32[4,8,64,128]{3,1,0,2:T(8,128)}), f32[4,8,64,128]{3,1,0,2:T(8,128)S(1)}, u32[]{:S(2)}, u32[]{:S(2)}) async-start(f32[4,8,64,128]{3,1,0,2:T(8,128)} %copy.24), calls=%async_computation | async-start | bytes 2097152 | tf_op jit(solution)/shard_map/all_to_all | solution.py:83
  248.9 1.2 convolution_bitcast_fusion.4
  250.4 1.5 fusion.3
  253.5 1.3 fusion.1
  254.8 1.6 copy.42
  256.4 7.3 %all-to-all-done = f32[4,8,64,128]{3,1,0,2:T(8,128)S(1)} async-done(((f32[4,8,64,128]{3,1,0,2:T(8,128)}), f32[4,8,64,128]{3,1,0,2:T(8,128)S(1)}, u32[]{:S(2)}, u32[]{:S(2)}) %all-to-all-start) | async-done | bytes 1048608 | tf_op jit(solution)/shard_map/all_to_all | solution.py:83
  263.8 3.7 %all-to-all-start.3 = ((f32[4,64,8,128]{3,2,0,1:T(8,128)}), f32[4,64,8,128]{3,2,0,1:T(8,128)S(1)}, u32[]{:S(2)}, u32[]{:S(2)}) async-start(f32[4,64,8,128]{3,2,0,1:T(8,128)} %copy.42), calls=%async_computation.3 | async-start | bytes 2097152 | tf_op jit(solution)/shard_map/all_to_all | solution.py:92
  267.4 1.2 convolution_bitcast_fusion.12
  269.0 1.5 fusion.8
  270.4 1.2 convolution_bitcast_fusion.10
  272.0 1.3 fusion.6
  273.3 1.6 copy.30
  274.9 7.5 %all-to-all-done.3 = f32[4,64,8,128]{3,2,0,1:T(8,128)S(1)} async-done(((f32[4,64,8,128]{3,2,0,1:T(8,128)}), f32[4,64,8,128]{3,2,0,1:T(8,128)S(1)}, u32[]{:S(2)}, u32[]{:S(2)}) %all-to-all-start.3) | async-done | bytes 1048608 | tf_op jit(solution)/shard_map/all_to_all | solution.py:92
  282.4 3.8 %all-to-all-start.1 = ((f32[4,64,8,128]{3,2,0,1:T(8,128)}), f32[4,64,8,128]{3,2,0,1:T(8,128)S(1)}, u32[]{:S(2)}, u32[]{:S(2)}) async-start(f32[4,64,8,128]{3,2,0,1:T(8,128)} %copy.30), calls=%async_computation.1 | async-start | bytes 2097152 | tf_op jit(solution)/shard_map/all_to_all | solution.py:92
  286.2 1.2 convolution_bitcast_fusion
  287.7 1.4 fusion
  290.5 10.5 %all-to-all-done.1 = f32[4,64,8,128]{3,2,0,1:T(8,128)S(1)} async-done(((f32[4,64,8,128]{3,2,0,1:T(8,128)}), f32[4,64,8,128]{3,2,0,1:T(8,128)S(1)}, u32[]{:S(2)}, u32[]{:S(2)}) %all-to-all-start.1) | async-done | bytes 1048608 | tf_op jit(solution)/shard_map/all_to_all | solution.py:92
  301.0 1.2 convolution_bitcast_fusion.8
  302.5 1.4 fusion.5
  (33 shorter events, 12.0 us)
Async XLA Ops:
  6.5 109.0 %all-gather.5.cloned.1.call-start = ((), (), s32[]{:S(2)}) async-start(), calls=%async_computation.4 | async-start | bytes 8650752 | tf_op jit(solution)/shard_map/all_gather | solution.py:15
  8.3 207.9 %all-gather.7.cloned.1.call-start = ((), (), s32[]{:S(2)}) async-start(), calls=%async_computation.5 | async-start | bytes 8650752 | tf_op jit(solution)/shard_map/all_gather | solution.py:15
  115.5 104.5 %copy-start = (f32[2,8,4096]{2,1,0:T(8,128)S(1)}, f32[2,8,4096]{2,1,0:T(8,128)}, u32[]{:S(2)}) copy-start(f32[2,8,4096]{2,1,0:T(8,128)} %param.1) | copy-start | bytes 786436
  226.2 19.0 %all-to-all-start.2 = ((f32[4,8,64,128]{3,1,0,2:T(8,128)}), f32[4,8,64,128]{3,1,0,2:T(8,128)S(1)}, u32[]{:S(2)}, u32[]{:S(2)}) async-start(f32[4,8,64,128]{3,1,0,2:T(8,128)} %copy.36), calls=%async_computation.2 | async-start | bytes 2097152 | tf_op jit(solution)/shard_map/all_to_all | solution.py:83
  245.1 18.6 %all-to-all-start = ((f32[4,8,64,128]{3,1,0,2:T(8,128)}), f32[4,8,64,128]{3,1,0,2:T(8,128)S(1)}, u32[]{:S(2)}, u32[]{:S(2)}) async-start(f32[4,8,64,128]{3,1,0,2:T(8,128)} %copy.24), calls=%async_computation | async-start | bytes 2097152 | tf_op jit(solution)/shard_map/all_to_all | solution.py:83
  263.8 18.6 %all-to-all-start.3 = ((f32[4,64,8,128]{3,2,0,1:T(8,128)}), f32[4,64,8,128]{3,2,0,1:T(8,128)S(1)}, u32[]{:S(2)}, u32[]{:S(2)}) async-start(f32[4,64,8,128]{3,2,0,1:T(8,128)} %copy.42), calls=%async_computation.3 | async-start | bytes 2097152 | tf_op jit(solution)/shard_map/all_to_all | solution.py:92
  282.4 18.6 %all-to-all-start.1 = ((f32[4,64,8,128]{3,2,0,1:T(8,128)}), f32[4,64,8,128]{3,2,0,1:T(8,128)S(1)}, u32[]{:S(2)}, u32[]{:S(2)}) async-start(f32[4,64,8,128]{3,2,0,1:T(8,128)} %copy.30), calls=%async_computation.1 | async-start | bytes 2097152 | tf_op jit(solution)/shard_map/all_to_all | solution.py:92
Sparse Core Ops, SparseCore 0:
  10.1 105.3 all-gather.4
  118.3 97.8 all-gather.6
